TPU v7x, 256 devices: a whole 4x4x8 slice. The times are simulated.
256 devices in a mesh: shards: 16 (over x, y), tensor: 4 (over z_hi, core), replica: 4 (over z_lo).
Axes of the slice: x: 4, y: 4, z: 8 (z_hi: 2, z_lo: 4; z = z_hi * 4 + z_lo), core: 2. Of those that a mesh axis runs over, the one named last changes fastest.
Arguments:
- activations: bfloat16 [262144, 1024], P(('shards', 'tensor', 'replica')), may hold values from -24 to 24
- grads_out: bfloat16 [262144, 1024], P(('shards', 'tensor', 'replica')), may hold values from -24 to 24
- grad_parts: float32 [64, 1024, 1024], P(('shards', 'replica'), None, 'tensor'), may hold values from -80 to 80
- old_factors: float32 [16, 128, 128], replicated, may hold values from -16 to 16, as said below
- block_owner: int32 [16], replicated, may hold values from 0 to 15, as said below
- weights: float32 [1024, 1024], P(('shards', 'replica'), 'tensor'), may hold values from -0.1875 to 0.1875
- momentum: float32 [1024, 1024], P(('shards', 'replica'), 'tensor'), may hold values from -4 to 4
Outputs:
- weights_next: float32 [1024, 1024], P(None, 'tensor')
- momentum_next: float32 [1024, 1024], P(('shards', 'replica'), 'tensor')
- next_factor_blocks: float32 [32, 128, 128], P('shards')
Inputs may be any that keep to these rules, and one draw needn't show every extreme that they name: `block_owner`: each shard index owns at most 2 of the 16 blocks, and some index owns exactly 2. `old_factors`: each block is symmetric and positive definite.
All inputs are finite; a program needn't handle non-finite values. Where the computation divides by a largest or mean magnitude, that divisor is 1e-20 or more.
Results may differ from a plain program's by a relative error of at most 0.0003.
Values sent between devices are 32-bit elements; how exact they have to be, the bound alone decides.
No kernel may reach another device: no remote copies, remote signals or barrier semaphores. Data moves between devices by JAX's collectives and lax.ppermute only.
A program may use at most 64 MiB of HBM per device.

v0:
```python
import jax
import jax.numpy as jnp
from jax import lax
from jax.sharding import PartitionSpec as P

NS_STEPS = 4
exact_mode = lax.Precision.HIGHEST
decay_rate = 0.75
damping = 0.1
damp_shift = 0.001
clip_norm = 256.0
momentum_rate = 0.9
step_rate = 0.05


def sample_stats(samples, block_size):
    sample_rows, width = samples.shape
    blocks = samples.reshape(sample_rows, width // block_size, block_size)
    return jnp.einsum("tnb,tnc->nbc", blocks, blocks, preferred_element_type=jnp.float32)


def build_slots(block_owner, capacity, slot_count):
    block_count = block_owner.shape[0]
    positions = jnp.arange(block_count, dtype=jnp.int32)
    earlier = (block_owner[:, None] == block_owner[None, :]) & (
        positions[None, :] < positions[:, None]
    )
    owner_slot_list = block_owner * capacity + jnp.sum(earlier.astype(jnp.int32), axis=1)
    return (owner_slot_list[None, :] == jnp.arange(slot_count, dtype=jnp.int32)[:, None]).astype(
        jnp.float32
    )


def newton_inverse(mixed_factor_blocks):
    block_size = mixed_factor_blocks.shape[-1]
    identity = jnp.eye(block_size, dtype=jnp.float32)
    traces = jnp.trace(mixed_factor_blocks, axis1=1, axis2=2)
    damped = (
        mixed_factor_blocks + (damping * traces / block_size + damp_shift)[:, None, None] * identity
    )
    bounds = jnp.max(jnp.sum(jnp.abs(damped), axis=2), axis=1)
    approx = identity[None, :, :] / bounds[:, None, None]
    for iteration in range(NS_STEPS):
        left_part = jnp.einsum("nab,nbc->nac", approx, damped, precision=exact_mode)
        approx = 2.0 * approx - jnp.einsum("nab,nbc->nac", left_part, approx, precision=exact_mode)
    return approx


def apply_right(left_part, right_inv, block_size):
    row_count, col_count = left_part.shape
    right_count = col_count // block_size
    return jnp.einsum(
        "rnb,nbc->rnc",
        left_part.reshape(row_count, right_count, block_size),
        right_inv,
        precision=exact_mode,
    ).reshape(row_count, col_count)


def body(activations, grads_out, grad_parts, old_factors, block_owner, weights, momentum):
    shard_count = lax.axis_size("shards")
    block_count = old_factors.shape[0]
    block_size = old_factors.shape[1]
    capacity = (block_count + shard_count - 1) // shard_count + 1
    slot_count = capacity * shard_count
    slot_table = build_slots(block_owner, capacity, slot_count)
    local_stats = jnp.concatenate(
        [sample_stats(activations, block_size), sample_stats(grads_out, block_size)], axis=0
    )
    packed = jnp.dot(
        slot_table, local_stats.reshape(block_count, block_size * block_size), precision=exact_mode
    )
    first_slot = lax.axis_index("shards") * capacity
    summed = lax.psum(packed, ("shards", "tensor", "replica"))
    owned = lax.dynamic_slice_in_dim(summed, first_slot, capacity, 0)
    sample_count = (
        activations.shape[0] * shard_count * lax.axis_size("tensor") * lax.axis_size("replica")
    )
    owned_table = lax.dynamic_slice_in_dim(slot_table, first_slot, capacity, 0)
    old_owned = jnp.dot(
        owned_table, old_factors.reshape(block_count, block_size * block_size), precision=exact_mode
    )
    mixed_factor_blocks = (
        decay_rate * old_owned + (1.0 - decay_rate) * (owned / sample_count)
    ).reshape(capacity, block_size, block_size)
    inverse_owned = newton_inverse(mixed_factor_blocks)
    start_blocks = jnp.zeros((block_count, block_size * block_size), jnp.float32)
    shard_piece = lax.all_gather(inverse_owned, "shards", axis=0, tiled=True)
    piece_rows = shard_piece.shape[0]
    rows_table = lax.slice_in_dim(slot_table, 0, piece_rows, axis=0)
    flat_piece = shard_piece.reshape(piece_rows, block_size * block_size)
    inverse_flat = start_blocks + jnp.einsum(
        "sb,sk->bk", rows_table, flat_piece, precision=exact_mode
    )
    inverse_blocks = inverse_flat.reshape(block_count, block_size, block_size)
    partial_grad = grad_parts[0]
    row_count, col_count = partial_grad.shape
    left_count = row_count // block_size
    right_count = col_count // block_size
    right_first = left_count + lax.axis_index("tensor") * right_count
    right_inv = lax.dynamic_slice_in_dim(inverse_blocks, right_first, right_count, 0)
    left_part = jnp.einsum(
        "nab,nbc->nac",
        inverse_blocks[:left_count],
        partial_grad.reshape(left_count, block_size, col_count),
        precision=exact_mode,
    ).reshape(row_count, col_count)
    precond = apply_right(left_part, right_inv, block_size)
    total_precond, total_grad = (
        lax.psum_scatter(precond, ("shards", "replica"), scatter_dimension=0, tiled=True),
        lax.psum_scatter(partial_grad, ("shards", "replica"), scatter_dimension=0, tiled=True),
    )
    alignment_sum = lax.psum(jnp.sum(total_precond * total_grad), ("shards", "tensor", "replica"))
    clip_scale = jnp.minimum(1.0, clip_norm / jnp.sqrt(alignment_sum))
    momentum_next = momentum_rate * momentum + clip_scale * total_precond
    weights_next = weights - step_rate * momentum_next
    gathered = lax.all_gather(weights_next, ("shards", "replica"), axis=0, tiled=True)
    return (gathered, momentum_next, mixed_factor_blocks)


def solution(mesh):
    placed = (
        P(("shards", "tensor", "replica"), None),
        P(("shards", "tensor", "replica"), None),
        P(("shards", "replica"), None, "tensor"),
        P(),
        P(),
        P(("shards", "replica"), "tensor"),
        P(("shards", "replica"), "tensor"),
    )
    return jax.shard_map(
        body,
        mesh=mesh,
        in_specs=placed,
        out_specs=(P(None, "tensor"), P(("shards", "replica"), "tensor"), P("shards", None, None)),
        check_vma=False,
    )
```

profile of v0, /device:TPU:94, one launch (start us, length us, event | category | flops | bytes accessed | tf_op | source)
XLA Modules:
  0.0 1458.4 jit_solution(3931337511195937440)
XLA Ops:
  8.0 0.0 copy-start
  8.0 0.0 all-reduce.2.cloned.1.call-start
  8.1 0.0 copy-start.7
  8.1 1.0 convert_reduce_fusion
  9.1 0.9 multiply_add_fusion.7
  10.0 0.0 copy-done
  10.0 1.1 fusion.4
  11.0 0.0 copy-done.7
  11.0 1.1 fusion.7
  12.2 0.1 pad_maximum_fusion
  12.2 0.0 copy-start.4
  12.3 2.8 fusion.10
  15.1 0.0 all-reduce.2.cloned.1.call-update
  15.1 0.0 all-gather.3.cloned.1.call-start
  15.2 259.1 %all-reduce.2.cloned.1.call-done = f32[32,16384]{1,0:T(8,128)} async-done(((f32[32,16384]{1,0:T(8,128)}), f32[32,16384]{1,0:T(8,128)}) %all-reduce.2.cloned.1.call-update) | async-done | bytes 2097168 | tf_op jit(solution)/shard_map/psum | solution.py:74
  274.3 0.0 copy-done.4
  274.3 2.3 select_reduce_fusion
  276.6 0.2 abs_reduce_fusion
  276.8 0.0 copy-start.3
  276.8 0.1 reduce_max.9
  276.9 0.3 fusion.20
  277.3 0.3 convolution_subtract_fusion.3
  277.6 0.3 fusion.25
  278.0 0.3 convolution_subtract_fusion.2
  278.3 0.3 fusion.24
  278.6 0.3 convolution_subtract_fusion.1
  278.9 0.3 fusion.23
  279.2 0.9 convolution_subtract_fusion
  280.1 0.0 all-gather.3.cloned.1.call-update
  280.2 0.0 reduce-scatter.5.cloned.1.call-start
  280.2 0.5 reduce-scatter.5.cloned.1.call-update
  280.7 0.0 copy-done.3
  280.8 0.2 reduce-scatter.3.cloned.1.call-start
  281.0 49.9 %all-gather.3.cloned.1.call-done = f32[32,128,128]{2,1,0:T(8,128)} async-done(((f32[2,128,128]{2,1,0:T(8,128)}), f32[32,128,128]{2,1,0:T(8,128)}) %all-gather.3.cloned.1.call-update) | async-done | bytes 2097168 | tf_op jit(solution)/shard_map/all_gather | solution.py:88
  330.9 0.0 copy-start.2
  330.9 3.6 fusion.1
  334.6 0.0 copy-done.2
  334.6 2.0 fusion.17
  336.7 2.7 reshape_reshape.3
  339.4 0.0 copy-start.1
  339.4 0.2 copy.41
  339.6 1.0 copy-done.1
  340.6 1.1 fusion.15
  341.7 0.0 copy-start.5
  341.7 0.0 copy-start.6
  341.7 1.3 copy.33
  343.0 0.0 reduce-scatter.3.cloned.1.call-update
  343.0 0.0 all-gather.5.cloned.1.call-start
  343.1 310.3 %reduce-scatter.5.cloned.1.call-done = f32[16,256]{1,0:T(8,128)} async-done(((f32[1024,256]{1,0:T(8,128)}), f32[16,256]{1,0:T(8,128)}) %reduce-scatter.5.cloned.1.call-update) | async-done | bytes 16400 | tf_op jit(solution)/shard_map/reduce_scatter | solution.py:111
  653.4 370.3 %reduce-scatter.3.cloned.1.call-done = f32[16,256]{1,0:T(8,128)} async-done(((f32[1024,256]{1,0:T(8,128)}), f32[16,256]{1,0:T(8,128)}) %reduce-scatter.3.cloned.1.call-update) | async-done | bytes 16400 | tf_op jit(solution)/shard_map/reduce_scatter | solution.py:110
  1023.7 1.3 multiply_reduce_fusion
  1025.0 72.1 %psum.15 = f32[]{:T(128)} all-reduce(f32[]{:T(128)} %multiply_reduce_fusion), channel_id=1, replica_groups=mesh['shards'=16,'tensor'=4,'replica'=4] {'shards','tensor','replica'}, use_global_device_ids=true, to_apply=%region_8.9 | all-reduce | flops 1 | bytes 8 | tf_op jit(solution)/shard_map/psum | solution.py:113
  1097.8 0.0 copy-done.5
  1097.9 0.0 copy-done.6
  1097.9 1.3 multiply_subtract_fusion
  1099.2 0.0 all-gather.5.cloned.1.call-update
  1099.2 349.3 %all-gather.5.cloned.1.call-done = f32[1024,256]{1,0:T(8,128)} async-done(((f32[16,256]{1,0:T(8,128)}), f32[1024,256]{1,0:T(8,128)}) %all-gather.5.cloned.1.call-update) | async-done | bytes 1048592 | tf_op jit(solution)/shard_map/all_gather | solution.py:117
  1448.5 2.3 copy.72
  (5 shorter events, 0.1 us)
Async XLA Ops:
  8.0 2.0 copy-start
  8.0 266.3 %all-reduce.2.cloned.1.call-start = ((), (), s32[]{:S(2)}) async-start(), calls=%async_computation.2 | async-start | bytes 4194304 | tf_op jit(solution)/shard_map/psum | solution.py:74
  8.1 3.0 copy-start.7
  12.2 262.0 %copy-start.4 = (f32[16,128,128]{2,1,0:T(8,128)S(1)}, f32[16,128,128]{2,1,0:T(8,128)}, u32[]{:S(2)}) copy-start(f32[16,128,128]{2,1,0:T(8,128)} %param.10) | copy-start | bytes 3145732
  15.1 315.9 %all-gather.3.cloned.1.call-start = ((), (), s32[]{:S(2)}) async-start(), calls=%async_computation.3 | async-start | bytes 2228224 | tf_op jit(solution)/shard_map/all_gather | solution.py:88
  276.8 3.9 copy-start.3
  280.2 373.2 %reduce-scatter.5.cloned.1.call-start = ((), (), s32[]{:S(2)}) async-start(), calls=%async_computation.5 | async-start | bytes 1064960 | tf_op jit(solution)/shard_map/reduce_scatter | solution.py:111
  280.8 742.9 %reduce-scatter.3.cloned.1.call-start = ((), (), s32[]{:S(2)}) async-start(), calls=%async_computation.4 | async-start | bytes 1064960 | tf_op jit(solution)/shard_map/reduce_scatter | solution.py:110
  330.9 3.7 copy-start.2
  339.4 1.2 copy-start.1
  341.7 756.2 %copy-start.5 = (f32[16,256]{1,0:T(8,128)S(1)}, f32[16,256]{1,0:T(8,128)}, u32[]{:S(2)}) copy-start(f32[16,256]{1,0:T(8,128)} %param.12) | copy-start | bytes 49156
  341.7 756.2 %copy-start.6 = (f32[16,256]{1,0:T(8,128)S(1)}, f32[16,256]{1,0:T(8,128)}, u32[]{:S(2)}) copy-start(f32[16,256]{1,0:T(8,128)} %param.13) | copy-start | bytes 49156
  343.0 1105.5 %all-gather.5.cloned.1.call-start = ((), (), s32[]{:S(2)}) async-start(), calls=%async_computation.6 | async-start | bytes 1064960 | tf_op jit(solution)/shard_map/all_gather | solution.py:117
Sparse Core Ops, SparseCore 0:
  15.2 259.0 all-reduce.1
  280.3 50.6 all-gather.2
Sparse Core Ops, SparseCore 1:
  283.1 370.2 reduce-scatter.4
  656.5 367.1 reduce-scatter.2
  1099.3 349.2 all-gather.4
where the time goes:
time: 1460 us
  waiting for transfers between devices  1340 us (92%)
  blocking collectives  72.1 us (5%)
  matrix products  17.2 us (1%)
  between operations  16.6 us (1%)
    reduce_scatter x1, waiting for transfers between devices, body(): lax.psum_scatter(precond, ('shards', 'replica'), scatter_dimension=0, til...  370 us
    all_gather x1, waiting for transfers between devices, body(): lax.all_gather(weights_next, ('shards', 'replica'), axis=0, tiled=True)  349 us
    reduce_scatter x1, waiting for transfers between devices, body(): lax.psum_scatter(partial_grad, ('shards', 'replica'), scatter_dimension=0...  310 us
    psum x1, waiting for transfers between devices, body(): summed = lax.psum(packed, ('shards', 'tensor', 'replica'))  259 us
    psum x1, blocking collectives, body(): lax.psum(jnp.sum(total_precond * total_grad), ('shards', 'tensor', 'repli...  72.1 us
    all_gather x1, waiting for transfers between devices, body(): shard_piece = lax.all_gather(inverse_owned, 'shards', axis=0, tiled=True)  49.9 us
  transfers between devices with their start and end apart: 5, of which 5 were waited for; matrix products, arithmetic and copies ran while one was open for 1% of the time, Pallas kernels for 0%

commit v1 on v0

--- a/solution.py
+++ b/solution.py
@@ -114,7 +114,15 @@
     clip_scale = jnp.minimum(1.0, clip_norm / jnp.sqrt(alignment_sum))
     momentum_next = momentum_rate * momentum + clip_scale * total_precond
     weights_next = weights - step_rate * momentum_next
-    gathered = lax.all_gather(weights_next, ("shards", "replica"), axis=0, tiled=True)
+    gathered = jnp.concatenate(
+        lax.all_to_all(
+            jnp.stack([weights_next] * lax.axis_size(("shards", "replica"))),
+            ("shards", "replica"),
+            0,
+            0,
+        ),
+        axis=0,
+    )
     return (gathered, momentum_next, mixed_factor_blocks)
 
 

time: 1460 us -> 1150 us (0.79)
  waiting for transfers between devices: 1340 us -> 990 us
  blocking collectives: 72.1 us -> 108 us
    all_gather x1 -> x0, waiting for transfers between devices: 349 us -> none  [body(): lax.all_gather(weights_next, ('shards', 'replica'), axis=0, tiled=True)]
    all_to_all x0 -> x1, blocking collectives: none -> 36 us  [body(): lax.all_to_all(jnp.stack([weights_next] * lax.axis_size(('shards', 'repli...]
  transfers between devices with their start and end apart: 5 -> 4, of which waited for: 5 -> 4; matrix products, arithmetic and copies ran while one was open for 1% -> 1% of each run, Pallas kernels for 0% -> 0%
where the time goes in v1:
time: 1150 us; the launch traced here: 1140 us
  waiting for transfers between devices  990 us (86%)
  blocking collectives  108 us (9%)
  matrix products  17.2 us (1%)
  between operations  16.4 us (1%)
    reduce_scatter x1, waiting for transfers between devices, body(): lax.psum_scatter(precond, ('shards', 'replica'), scatter_dimension=0, til...  370 us
    reduce_scatter x1, waiting for transfers between devices, body(): lax.psum_scatter(partial_grad, ('shards', 'replica'), scatter_dimension=0...  310 us
    psum x1, waiting for transfers between devices, body(): summed = lax.psum(packed, ('shards', 'tensor', 'replica'))  259 us
    psum x1, blocking collectives, body(): lax.psum(jnp.sum(total_precond * total_grad), ('shards', 'tensor', 'repli...  72.1 us
    all_gather x1, waiting for transfers between devices, body(): shard_piece = lax.all_gather(inverse_owned, 'shards', axis=0, tiled=True)  49.9 us
    all_to_all x1, blocking collectives, body(): lax.all_to_all(jnp.stack([weights_next] * lax.axis_size(('shards', 'repli...  36 us
  transfers between devices with their start and end apart: 4, of which 4 were waited for; matrix products, arithmetic and copies ran while one was open for 1% of the time, Pallas kernels for 0%

profile of v1, /device:TPU:94, one launch (start us, length us, event | category | flops | bytes accessed | tf_op | source)
XLA Modules:
  0.0 1143.7 jit_solution(13893582625262396883)
XLA Ops:
  8.0 0.0 copy-start
  8.0 0.0 all-reduce.2.cloned.1.call-start
  8.1 0.0 copy-start.7
  8.1 1.0 convert_reduce_fusion
  9.1 0.9 multiply_add_fusion.7
  10.0 0.0 copy-done
  10.0 1.1 fusion.4
  11.0 0.0 copy-done.7
  11.0 1.1 fusion.7
  12.2 0.1 pad_maximum_fusion
  12.2 0.0 copy-start.4
  12.3 2.8 fusion.10
  15.1 0.0 all-reduce.2.cloned.1.call-update
  15.1 0.0 all-gather.2.cloned.1.call-start
  15.2 259.1 %all-reduce.2.cloned.1.call-done = f32[32,16384]{1,0:T(8,128)} async-done(((f32[32,16384]{1,0:T(8,128)}), f32[32,16384]{1,0:T(8,128)}) %all-reduce.2.cloned.1.call-update) | async-done | bytes 2097168 | tf_op jit(solution)/shard_map/psum | solution.py:74
  274.3 0.0 copy-done.4
  274.3 2.3 select_reduce_fusion
  276.6 0.2 abs_reduce_fusion
  276.8 0.0 copy-start.3
  276.8 0.1 reduce_max.9
  276.9 0.3 fusion.20
  277.3 0.3 convolution_subtract_fusion.3
  277.6 0.3 fusion.25
  278.0 0.3 convolution_subtract_fusion.2
  278.3 0.3 fusion.24
  278.6 0.3 convolution_subtract_fusion.1
  278.9 0.3 fusion.23
  279.2 0.9 convolution_subtract_fusion
  280.1 0.0 all-gather.2.cloned.1.call-update
  280.2 0.0 reduce-scatter.5.cloned.1.call-start
  280.2 0.5 reduce-scatter.5.cloned.1.call-update
  280.7 0.0 copy-done.3
  280.8 0.2 reduce-scatter.3.cloned.1.call-start
  281.0 49.9 %all-gather.2.cloned.1.call-done = f32[32,128,128]{2,1,0:T(8,128)} async-done(((f32[2,128,128]{2,1,0:T(8,128)}), f32[32,128,128]{2,1,0:T(8,128)}) %all-gather.2.cloned.1.call-update) | async-done | bytes 2097168 | tf_op jit(solution)/shard_map/all_gather | solution.py:88
  330.9 0.0 copy-start.2
  330.9 3.6 fusion.1
  334.6 0.0 copy-done.2
  334.6 2.0 fusion.17
  336.7 2.7 reshape_reshape.3
  339.4 0.0 copy-start.1
  339.4 0.2 copy.41
  339.6 1.0 copy-done.1
  340.6 1.1 fusion.15
  341.7 0.0 copy-start.5
  341.7 0.0 copy-start.6
  341.7 1.3 copy.33
  343.0 0.0 reduce-scatter.3.cloned.1.call-update
  343.0 310.4 %reduce-scatter.5.cloned.1.call-done = f32[16,256]{1,0:T(8,128)} async-done(((f32[1024,256]{1,0:T(8,128)}), f32[16,256]{1,0:T(8,128)}) %reduce-scatter.5.cloned.1.call-update) | async-done | bytes 16400 | tf_op jit(solution)/shard_map/reduce_scatter | solution.py:111
  653.4 370.3 %reduce-scatter.3.cloned.1.call-done = f32[16,256]{1,0:T(8,128)} async-done(((f32[1024,256]{1,0:T(8,128)}), f32[16,256]{1,0:T(8,128)}) %reduce-scatter.3.cloned.1.call-update) | async-done | bytes 16400 | tf_op jit(solution)/shard_map/reduce_scatter | solution.py:110
  1023.7 1.3 multiply_reduce_fusion
  1025.0 72.1 %psum.15 = f32[]{:T(128)} all-reduce(f32[]{:T(128)} %multiply_reduce_fusion), channel_id=1, replica_groups=mesh['shards'=16,'tensor'=4,'replica'=4] {'shards','tensor','replica'}, use_global_device_ids=true, to_apply=%region_8.9 | all-reduce | flops 1 | bytes 8 | tf_op jit(solution)/shard_map/psum | solution.py:113
  1097.9 0.0 copy-done.5
  1097.9 0.0 copy-done.6
  1097.9 1.3 multiply_subtract_fusion
  1099.2 0.1 stack.2
  1099.3 36.0 %all_to_all.5 = f32[64,16,256]{2,1,0:T(8,128)S(1)} all-to-all(f32[64,16,256]{2,1,0:T(8,128)S(1)} %stack.2), channel_id=1, replica_groups=mesh['shards'=16,'tensor'=4,'replica'=4] {'shards','replica'}, dimensions={0} | all-to-all | bytes 2097152 | tf_op jit(solution)/shard_map/all_to_all | solution.py:118
  1135.3 1.0 copy.72
  (5 shorter events, 0.1 us)
Async XLA Ops:
  8.0 2.0 copy-start
  8.0 266.3 %all-reduce.2.cloned.1.call-start = ((), (), s32[]{:S(2)}) async-start(), calls=%async_computation.3 | async-start | bytes 4194304 | tf_op jit(solution)/shard_map/psum | solution.py:74
  8.1 3.0 copy-start.7
  12.2 262.0 %copy-start.4 = (f32[16,128,128]{2,1,0:T(8,128)S(1)}, f32[16,128,128]{2,1,0:T(8,128)}, u32[]{:S(2)}) copy-start(f32[16,128,128]{2,1,0:T(8,128)} %param.10) | copy-start | bytes 3145732
  15.1 315.9 %all-gather.2.cloned.1.call-start = ((), (), s32[]{:S(2)}) async-start(), calls=%async_computation.4 | async-start | bytes 2228224 | tf_op jit(solution)/shard_map/all_gather | solution.py:88
  276.8 3.9 copy-start.3
  280.2 373.2 %reduce-scatter.5.cloned.1.call-start = ((), (), s32[]{:S(2)}) async-start(), calls=%async_computation.6 | async-start | bytes 1064960 | tf_op jit(solution)/shard_map/reduce_scatter | solution.py:111
  280.8 742.9 %reduce-scatter.3.cloned.1.call-start = ((), (), s32[]{:S(2)}) async-start(), calls=%async_computation.5 | async-start | bytes 1064960 | tf_op jit(solution)/shard_map/reduce_scatter | solution.py:110
  330.9 3.7 copy-start.2
  339.4 1.2 copy-start.1
  341.7 756.2 %copy-start.5 = (f32[16,256]{1,0:T(8,128)S(1)}, f32[16,256]{1,0:T(8,128)}, u32[]{:S(2)}) copy-start(f32[16,256]{1,0:T(8,128)} %param.12) | copy-start | bytes 49156
  341.7 756.2 %copy-start.6 = (f32[16,256]{1,0:T(8,128)S(1)}, f32[16,256]{1,0:T(8,128)}, u32[]{:S(2)}) copy-start(f32[16,256]{1,0:T(8,128)} %param.13) | copy-start | bytes 49156
Sparse Core Ops, SparseCore 0:
  15.2 259.0 all-reduce.1
  280.3 50.6 all-gather.1
Sparse Core Ops, SparseCore 1:
  283.1 370.2 reduce-scatter.4
  656.5 367.1 reduce-scatter.2
